TPU v7x, 256 devices: a whole 4x4x8 slice. The times are simulated.
256 devices in a mesh: req: 32 (over z_hi, y, x), tp: 8 (over z_lo, core).
Axes of the slice: x: 4, y: 4, z: 8 (z_hi: 2, z_lo: 4; z = z_hi * 4 + z_lo), core: 2. Of those that a mesh axis runs over, the one named last changes fastest.
Arguments:
- queries: bfloat16 [64, 256, 16, 256], P('req', None, 'tp'), may hold values from -6 to 6
- suffix_kv: bfloat16 [64, 256, 8, 512], P('req', None, 'tp'), may hold values from -6 to 6
- prefix_kv: bfloat16 [32, 1024, 8, 512], P('req', None, 'tp'), may hold values from -6 to 6
- out_weight: bfloat16 [4096, 3584], P('tp'), may hold values from -0.09375 to 0.09375
- residual: bfloat16 [64, 256, 3584], P('req', None, 'tp'), may hold values from -6 to 6
- norm_gain: float32 [3584], P('tp'), may hold values from 0.5 to 1.5
- suffix_len: int32 [64], replicated, may hold values from 1 to 256, 8192 in all
- member: int32 [64], replicated, may hold values from 0 to 63, each once
- owner: int32 [8], replicated, may hold values from 0 to 31, as said below
- assign: int32 [64], replicated, may hold values from 0 to 63, each once
Outputs:
- block_out: bfloat16 [64, 256, 3584], P('req', None, 'tp')
Inputs may be any that keep to these rules, and one draw needn't show every extreme that they name: `owner`: distinct req indices.
All inputs are finite; a program needn't handle non-finite values.
Results may differ from a plain program's by a relative error of at most 0.011.
Values may be sent and summed in bfloat16 or wider, within the bound.
A program may use at most 64 MiB of HBM per device.

v0:
```python
import jax
import jax.numpy as jnp
from jax import lax
from jax.sharding import PartitionSpec as P

D = 3584


def padded_to(lines, size):
    spare = -lines.shape[0] % size
    if not spare:
        return lines
    return jnp.concatenate([lines, jnp.zeros((spare, *lines.shape[1:]), lines.dtype)])


def total_of(value, axis):
    lines = value.reshape(-1, *value.shape[1:][-1:])
    own = lax.psum_scatter(
        padded_to(lines, lax.axis_size(axis)), axis, scatter_dimension=0, tiled=True
    )
    whole = lax.all_gather(own, axis).reshape(-1, *lines.shape[1:])
    return lax.slice_in_dim(whole, 0, len(lines)).reshape(value.shape)


def attend(query, keys, allowed):
    head_dim = query.shape[-1]
    key_part = keys[..., :head_dim]
    value_part = keys[..., head_dim:]
    scores = (
        jnp.einsum("bsgrd,bkgd->bgrsk", query, key_part, preferred_element_type=jnp.float32)
        * 0.0625
    )
    capped = 50.0 * jnp.tanh(scores / 50.0)
    weights = jnp.where(allowed, jnp.exp(capped), 0.0)
    total = jnp.sum(weights, -1)
    numer = jnp.einsum(
        "bgrsk,bkgd->bsgrd",
        weights.astype(jnp.bfloat16),
        value_part,
        preferred_element_type=jnp.float32,
    )
    return (numer, jnp.moveaxis(total, 3, 1))


def local(
    queries,
    suffix_kv,
    prefix_kv,
    out_weight,
    residual,
    norm_gain,
    suffix_len,
    member,
    owner,
    assign,
):
    req_local, seq_slots, heads_local, head_dim = queries.shape
    kv_local = suffix_kv.shape[2]
    query = queries.reshape(req_local, seq_slots, kv_local, heads_local // kv_local, head_dim)
    device = lax.axis_index("req")
    requests = lax.dynamic_slice_in_dim(assign, device * req_local, req_local)
    lookup = requests[:, None] == jnp.arange(suffix_len.shape[0])[None, :]
    lengths = jnp.sum(jnp.where(lookup, suffix_len[None, :], 0), 1)
    group_of = jnp.sum(jnp.where(lookup, member[None, :], 0), 1) // (
        suffix_len.shape[0] // owner.shape[0]
    )
    positions = jnp.arange(seq_slots)
    own_mask = (positions[None, :] <= positions[:, None])[None] & (
        positions[None, None, :] < lengths[:, None, None]
    )
    prefix_slab = prefix_kv[0]
    chosen = jnp.zeros((req_local,) + prefix_slab.shape, prefix_slab.dtype)
    holds = owner == device
    placed = jnp.where(holds[:, None, None, None], prefix_slab[None].astype(jnp.float32), 0.0)
    slabs = total_of(placed.astype(jnp.bfloat16), "req").astype(jnp.float32).astype(jnp.bfloat16)
    for number in range(owner.shape[0]):
        chosen = jnp.where((group_of == number)[:, None, None, None], slabs[number][None], chosen)
    prefix_numer, prefix_total = attend(query, chosen, jnp.ones((1, 1, 1, 1, 1), bool))
    suffix_numer, suffix_total = attend(query, suffix_kv, own_mask[:, None, None])
    numer = prefix_numer + suffix_numer
    total = prefix_total + suffix_total
    attended = (
        (numer / total[..., None])
        .astype(jnp.bfloat16)
        .reshape(req_local * seq_slots, heads_local * head_dim)
    )
    partial_value = jnp.dot(attended, out_weight, preferred_element_type=jnp.float32)
    width_local = residual.shape[-1]
    mine = lax.psum_scatter(
        partial_value.astype(jnp.bfloat16), "tp", scatter_dimension=1, tiled=True
    ).astype(jnp.float32)
    squares = lax.psum(jnp.sum(mine * mine, -1, keepdims=True), "tp")
    scale = lax.rsqrt(squares / D + 1e-06)
    normed = mine * scale * norm_gain[None, :]
    stream = residual.reshape(req_local * seq_slots, width_local).astype(jnp.float32)
    return (stream + normed).astype(jnp.bfloat16).reshape(residual.shape)


def solution(mesh):
    in_specs = (
        P("req", None, "tp", None),
        P("req", None, "tp", None),
        P("req", None, "tp", None),
        P("tp", None),
        P("req", None, "tp"),
        P("tp"),
        P(),
        P(),
        P(),
        P(),
    )
    out_specs = P("req", None, "tp")
    return jax.shard_map(local, mesh=mesh, in_specs=in_specs, out_specs=out_specs, check_vma=False)
```

profile of v0, /device:TPU:1, one launch (start us, length us, event | category | flops | bytes accessed | tf_op | source)
XLA Modules:
  0.0 540.9 jit_solution(16213651043490003993)
XLA Ops:
  6.5 0.7 broadcast_compare_fusion.4
  7.3 0.1 broadcast_bitcast_fusion
  7.3 6.0 %fusion = bf16[8192,512]{1,0:T(8,128)(2,1)} fusion(bf16[1024,512]{1,0:T(8,128)(2,1)} %bitcast.102, pred[8192]{0:T(1024)(128)(4,1)S(1)} %bitcast.104), kind=kLoop, calls=%fused_computation.1 | loop fusion | flops 4194304 | bytes 9445376 | tf_op jit(solution)/shard_map/convert_element_type | solution.py:75
  13.4 0.0 reduce-scatter.3.cloned.1.call-update
  13.4 0.0 all-gather.3.cloned.1.call-start
  13.4 261.2 %reduce-scatter.3.cloned.1.call-done = bf16[256,512]{1,0:T(8,128)(2,1)} async-done(((bf16[8192,512]{1,0:T(8,128)(2,1)}), bf16[256,512]{1,0:T(8,128)(2,1)}) %reduce-scatter.3.cloned.1.call-update) | async-done | bytes 262160 | tf_op jit(solution)/shard_map/reduce_scatter | solution.py:18
  274.7 0.0 all-gather.3.cloned.1.call-update
  274.7 0.0 reduce-scatter.5.cloned.1.call-start
  274.7 0.1 dynamic_slice.3
  274.8 0.0 copy-done.4
  274.8 0.2 select_reduce_fusion
  275.1 0.1 iota_compare_fusion.1
  275.1 0.1 broadcast_and_fusion
  275.3 0.5 fusion.25
  275.8 178.2 %all-gather.3.cloned.1.call-done = bf16[8192,512]{1,0:T(8,128)(2,1)} async-done(((bf16[256,512]{1,0:T(8,128)(2,1)}), bf16[8192,512]{1,0:T(8,128)(2,1)}) %all-gather.3.cloned.1.call-update) | async-done | bytes 8388624 | tf_op jit(solution)/shard_map/all_gather | solution.py:21
  454.1 3.8 fusion.24
  457.8 0.9 select_select_fusion
  458.7 1.3 bitcast_reduce_fusion
  460.1 1.5 fusion.2
  461.6 0.3 divide_convert_fusion
  461.9 0.5 copy.41
  462.4 0.1 copy.55
  462.5 5.9 %convolution_convert_fusion = bf16[512,3584]{0,1:T(8,128)(2,1)} fusion(bf16[512,512]{1,0:T(8,128)(2,1)S(1)} %bitcast.103, bf16[512,3584]{1,0:T(8,128)(2,1)} %param.13), kind=kOutput, calls=%fused_computation.2 | convolution fusion | flops 1880883200 | bytes 7864320 | tf_op jit(solution)/shard_map/dot_general | solution.py:87
  468.4 0.0 reduce-scatter.5.cloned.1.call-update
  468.5 1.0 copy-done.1
  469.4 0.1 convert_bitcast_fusion
  469.5 0.1 copy.53
  469.6 45.5 %reduce-scatter.5.cloned.1.call-done = bf16[512,448]{0,1:T(8,128)(2,1)} async-done(((bf16[512,3584]{0,1:T(8,128)(2,1)}), bf16[512,448]{0,1:T(8,128)(2,1)}) %reduce-scatter.5.cloned.1.call-update) | async-done | bytes 458768 | tf_op jit(solution)/shard_map/reduce_scatter | solution.py:89
  515.2 1.2 fusion.14
  516.3 16.0 %psum.7 = f32[512,1]{0,1:T(1,128)S(1)} all-reduce(f32[512,1]{0,1:T(1,128)S(1)} %bitcast.106), channel_id=1, replica_groups=mesh['req'=32,'tp'=8] {'tp'}, use_global_device_ids=true, to_apply=%region_7.8 | all-reduce | flops 512 | bytes 4096 | tf_op jit(solution)/shard_map/psum | solution.py:92
  532.4 1.2 fusion.17
  533.6 0.8 copy.66
  (19 shorter events, 0.1 us)
Async XLA Ops:
  6.5 268.8 %copy-start = (bf16[2,256,2,256]{3,2,1,0:T(2,128)(2,1)S(1)}, bf16[2,256,2,256]{3,2,1,0:T(2,128)(2,1)}, u32[]{:S(2)}) copy-start(bf16[2,256,2,256]{3,2,1,0:T(2,128)(2,1)} %param.10) | copy-start | bytes 1572868
  6.5 268.1 %reduce-scatter.3.cloned.1.call-start = ((), (), s32[]{:S(2)}) async-start(), calls=%async_computation.2 | async-start | bytes 8650752 | tf_op jit(solution)/shard_map/reduce_scatter | solution.py:18
  13.4 261.4 %copy-start.6 = (s32[64]{0:T(128)S(1)}, s32[64]{0:T(128)}, u32[]{:S(2)}) copy-start(s32[64]{0:T(128)} %param.19) | copy-start | bytes 772
  13.4 261.5 %copy-start.3 = (s32[64]{0:T(128)S(1)}, s32[64]{0:T(128)}, u32[]{:S(2)}) copy-start(s32[64]{0:T(128)} %param.16) | copy-start | bytes 772
  13.4 261.5 %copy-start.4 = (s32[64]{0:T(128)S(1)}, s32[64]{0:T(128)}, u32[]{:S(2)}) copy-start(s32[64]{0:T(128)} %param.17) | copy-start | bytes 772
  13.4 261.9 %copy-start.5 = (bf16[2,256,1,512]{3,1,2,0:T(8,128)(2,1)S(1)}, bf16[2,256,1,512]{3,1,2,0:T(8,128)(2,1)}, u32[]{:S(2)}) copy-start(bf16[2,256,1,512]{3,1,2,0:T(8,128)(2,1)} %param.11) | copy-start | bytes 1572868
  13.4 440.7 %all-gather.3.cloned.1.call-start = ((), (), s32[]{:S(2)}) async-start(), calls=%async_computation.4 | async-start | bytes 8650752 | tf_op jit(solution)/shard_map/all_gather | solution.py:21
  274.7 240.5 %reduce-scatter.5.cloned.1.call-start = ((), (), s32[]{:S(2)}) async-start(), calls=%async_computation.3 | async-start | bytes 4128768 | tf_op jit(solution)/shard_map/reduce_scatter | solution.py:89
  468.4 1.0 copy-start.1
  468.4 63.9 %copy-start.2 = (f32[448]{0:T(512)S(1)}, f32[448]{0:T(512)}, u32[]{:S(2)}) copy-start(f32[448]{0:T(512)} %param.15) | copy-start | bytes 5380
Sparse Core Ops, SparseCore 0:
  13.5 261.0 reduce-scatter.2
  278.2 175.8 all-gather.2
  468.6 46.5 reduce-scatter.4
where the time goes:
time: 541 us
  waiting for transfers between devices  485 us (90%)
  blocking collectives  16 us (3%)
  between operations  13.3 us (2%)
  other arithmetic  10.5 us (2%)
  matrix products  9.64 us (2%)
  local copies, waits for them, and re-layouts  6.37 us (1%)
    reduce_scatter x1, waiting for transfers between devices, total_of(): lax.psum_scatter(padded_to(lines, lax.axis_size(axis)), axis, scatter_dim...  261 us
    all_gather x1, waiting for transfers between devices, total_of(): whole = lax.all_gather(own, axis).reshape(-1, *lines.shape[1:])  178 us
    reduce_scatter x1, waiting for transfers between devices, local(): lax.psum_scatter(partial_value.astype(jnp.bfloat16), 'tp', scatter_dimens...  45.5 us
    psum x1, blocking collectives, local(): squares = lax.psum(jnp.sum(mine * mine, -1, keepdims=True), 'tp')  16 us
  transfers between devices with their start and end apart: 3, of which 3 were waited for; matrix products, arithmetic and copies ran while one was open for 0% of the time, Pallas kernels for 0%

commit v1 on v0

v1 whole, which is shorter than its diff:
```python
import jax
import jax.numpy as jnp
from jax import lax
from jax.experimental import pallas as pl
from jax.experimental.pallas import tpu as pltpu
from jax.sharding import PartitionSpec as P

D = 3584
MESH = pl.DeviceIdType.MESH
CHUNKS = 4
PLANE = 16
ROWS = 1024 // PLANE // CHUNKS
BF = jnp.bfloat16
F32 = jnp.float32
NT = (((1,), (1,)), ((), ()))
COLS = 448


def kernel(
    suffix_len, member, owner, assign,
    q_hbm, suf_hbm, pre_hbm, w_hbm, res_hbm, gain_hbm,
    out,
    got, both, out_kv, kv,
    q, suf, w, wt, wtr, res, gain, acc, tot, att, attr,
    part, mid, own, landed, sq, sqr, table,
    local_sem, own_sem, p1s, p1r, zs, zr, p2s, p2r, ws, wr, ats, atr, rs, rr, ss, sr,
):
    req = lax.axis_index("req")
    tp = lax.axis_index("tp")
    half = req // PLANE
    me = req % PLANE
    mx, my = me % 4, me // 4
    z, core = tp // 2, tp % 2
    other_half = 1 - half
    partner = tp + 1 - 2 * core
    base = half * PLANE

    def away(d):
        return (my + d // 4) % 4 * 4 + (mx + d % 4) % 4

    def local(i, src, dst):
        return pltpu.make_async_copy(src, dst, local_sem.at[i])

    loads = [
        local(0, q_hbm, q), local(1, suf_hbm, suf), local(2, w_hbm, w),
        local(3, res_hbm, res), local(4, gain_hbm, gain),
    ]

    barrier = pltpu.get_barrier_semaphore()

    @pl.loop(1, PLANE)
    def _(d):
        pl.semaphore_signal(barrier, inc=1, device_id=(base + away(d), tp), device_id_type=MESH)

    @pl.loop(1, 8)
    def _(d):
        pl.semaphore_signal(barrier, inc=1, device_id=(req, (tp + d) % 8), device_id_type=MESH)

    pl.semaphore_signal(
        barrier, inc=1, device_id=(other_half * PLANE + me, tp), device_id_type=MESH
    )
    for load in loads:
        load.start()
    mine = [
        pltpu.make_async_copy(pre_hbm.at[me, c], got[c].at[me], own_sem.at[c])
        for c in range(CHUNKS)
    ]
    for copy in mine:
        copy.start()
    pl.semaphore_wait(barrier, 23)

    def first(c, d):
        to = away(d)
        return pltpu.make_async_remote_copy(
            src_ref=pre_hbm.at[to, c], dst_ref=got[c].at[me],
            send_sem=p1s.at[c, d], recv_sem=p1r.at[c, d],
            device_id=(base + to, tp), device_id_type=MESH,
        )

    for c in range(CHUNKS):
        @pl.loop(1, PLANE)
        def _(d, c=c):
            first(c, d).start()

    @pl.loop(0, PLANE)
    def _(d):
        for s in range(2):
            group = member[assign[(base + away(d)) * 2 + s]] // 8
            apart = owner[group] // PLANE - half
            table[2 * d + s] = group + 8 * apart * apart

    def across(c):
        return pltpu.make_async_remote_copy(
            src_ref=both[c].at[pl.ds(0, 8)], dst_ref=both[c].at[pl.ds(8, 8)],
            send_sem=zs.at[c], recv_sem=zr.at[c],
            device_id=(other_half * PLANE + me, tp), device_id_type=MESH,
        )

    def send_across(c):
        mine[c].wait()

        @pl.loop(1, PLANE)
        def _(d):
            first(c, d).wait_recv()

        for g in range(8):
            both[c][g] = got[c][owner[g] % PLANE]
        across(c).start()

    def third(c, s, d):
        return pltpu.make_async_remote_copy(
            src_ref=out_kv[c][s].at[d], dst_ref=kv[c][s].at[me],
            send_sem=p2s.at[c, s, d], recv_sem=p2r.at[c, s, d],
            device_id=(base + away(d), tp), device_id_type=MESH,
        )

    def send_needed(c):
        across(c).wait_recv()
        for s in range(2):
            kv[c][s][me] = both[c][table[s]]

            @pl.loop(1, PLANE)
            def _(d, s=s):
                out_kv[c][s][d] = both[c][table[2 * d + s]]

            @pl.loop(1, PLANE)
            def _(d, s=s):
                third(c, s, d).start()

    def weigh(s, keys):
        scores = lax.dot_general(q[s], keys, NT, preferred_element_type=F32)
        return jnp.exp(50.0 * jnp.tanh(scores * 0.00125))

    def lanes(weights):
        total = weights[:, :128]
        for i in range(1, weights.shape[1] // 128):
            total = total + weights[:, 128 * i : 128 * (i + 1)]
        return total

    def attend_suffix(s):
        length = suffix_len[assign[req * 2 + s]]
        row = lax.broadcasted_iota(jnp.int32, (512, 256), 0) % 256
        key = lax.broadcasted_iota(jnp.int32, (512, 256), 1)
        weights = weigh(s, suf[s, :, :256])
        weights = jnp.where((key <= row) & (key < length), weights, 0.0)
        acc[s] = jnp.dot(weights.astype(BF), suf[s, :, 256:], preferred_element_type=F32)
        tot[s] = lanes(weights)

    def attend(c, s):
        @pl.loop(1, PLANE)
        def _(d):
            third(c, s, d).wait_recv()

        both_parts = kv[c][s][...].reshape(PLANE * ROWS, 512)
        weights = weigh(s, both_parts[:, :256])
        acc[s] += jnp.dot(weights.astype(BF), both_parts[:, 256:], preferred_element_type=F32)
        tot[s] += lanes(weights)

    def to_partner(i):
        return pltpu.make_async_remote_copy(
            src_ref=wt.at[pl.ds(pl.multiple_of(896 * i + COLS * (1 - core), 64), COLS)],
            dst_ref=wtr.at[pl.ds(COLS * i, COLS)],
            send_sem=ws.at[i], recv_sem=wr.at[i],
            device_id=(req, partner), device_id_type=MESH,
        )

    def turn_weights():
        loads[2].wait()
        for i in range(4):
            wt[896 * i : 896 * (i + 1), :] = w[:, 896 * i : 896 * (i + 1)].T
        for i in range(4):
            to_partner(i).start()

    def share(s):
        return pltpu.make_async_remote_copy(
            src_ref=att.at[s], dst_ref=attr.at[s], send_sem=ats.at[s], recv_sem=atr.at[s],
            device_id=(req, partner), device_id_type=MESH,
        )

    near, far, cross = z + 1 - 2 * (z % 2), (z + 2) % 4, 3 - z
    middle = ((z + 1) // 2) % 2
    ahead = near + middle * (cross - near)

    def to_near(s):
        return pltpu.make_async_remote_copy(
            src_ref=part.at[s, 1], dst_ref=landed.at[s, 1],
            send_sem=rs.at[s, 1], recv_sem=rr.at[s, 1],
            device_id=(req, 2 * near + core), device_id_type=MESH,
        )

    def to_far(s):
        return pltpu.make_async_remote_copy(
            src_ref=part.at[s, 2], dst_ref=landed.at[s, 2],
            send_sem=rs.at[s, 2], recv_sem=rr.at[s, 2],
            device_id=(req, 2 * far + core), device_id_type=MESH,
        )

    def to_ahead(s):
        return pltpu.make_async_remote_copy(
            src_ref=part.at[s, 0], dst_ref=landed.at[s, 3 * middle],
            send_sem=rs.at[s, 0], recv_sem=rr.at[s, 3 * middle],
            device_id=(req, 2 * ahead + core), device_id_type=MESH,
        )

    def arrived(s, i):
        return pltpu.make_async_remote_copy(
            src_ref=part.at[s, 0], dst_ref=landed.at[s, i],
            send_sem=rs.at[s, 0], recv_sem=rr.at[s, i],
            device_id=(req, 2 * near + core), device_id_type=MESH,
        )

    def project(s):
        total = jnp.sum(tot[s], axis=1, keepdims=True)
        value = (acc[s] / total).astype(BF)
        att[s, :, :256] = value[:256]
        att[s, :, 256:] = value[256:]
        share(s).start()

        def here(block):
            start = pl.multiple_of(896 * block + COLS * core, 64)
            return lax.dot_general(
                wt[pl.ds(start, COLS), :], att[s], NT, preferred_element_type=F32
            )

        def there(block):
            start = pl.multiple_of(COLS * block, 64)
            return lax.dot_general(
                wtr[pl.ds(start, COLS), :], attr[s], NT, preferred_element_type=F32
            )

        own[s] = here(cross)
        mid[s] = here(far)
        share(s).wait_recv()
        part[s, 0] = (own[s] + there(cross)).astype(BF)
        to_ahead(s).start()
        mid[s] += there(far)

        @pl.when(middle == 0)
        def _():
            part[s, 2] = mid[s].astype(BF)
            to_far(s).start()

        part[s, 1] = (here(near) + there(near)).astype(BF)
        to_near(s).start()
        own[s] = here(z) + there(z)

        @pl.when(middle == 1)
        def _():
            arrived(s, 0).wait_recv()
            part[s, 2] = (mid[s] + landed[s, 0].astype(F32)).astype(BF)
            to_far(s).start()

    def tell(s, d):
        return pltpu.make_async_remote_copy(
            src_ref=sq.at[s], dst_ref=sqr.at[s, d], send_sem=ss.at[s, d], recv_sem=sr.at[s, d],
            device_id=(req, (tp + d) % 8), device_id_type=MESH,
        )

    def gather_sums(s):
        @pl.when(middle == 1)
        def _():
            arrived(s, 3).wait_recv()
            own[s] += landed[s, 3].astype(F32)

        to_near(s).wait_recv()
        to_far(s).wait_recv()
        value = own[s] + landed[s, 1].astype(F32) + landed[s, 2].astype(F32)
        own[s] = value
        sq[s] = jnp.broadcast_to(jnp.sum(value * value, axis=0, keepdims=True), (8, 256))

        @pl.loop(1, 8)
        def _(d):
            tell(s, d).start()

    def finish(s):
        @pl.loop(1, 8)
        def _(d):
            tell(s, d).wait_recv()

        squares = sq[s]
        for d in range(1, 8):
            squares = squares + sqr[s, d]
        scale = lax.rsqrt(squares[:1] / D + 1e-06)
        out[s] = (res[s].astype(F32) + own[s] * scale * gain[...]).astype(BF)

    loads[0].wait()
    loads[1].wait()
    attend_suffix(0)
    send_across(0)
    attend_suffix(1)
    send_across(1)
    turn_weights()
    send_across(2)
    send_needed(0)
    send_across(3)
    send_needed(1)
    attend(0, 0)
    attend(0, 1)
    send_needed(2)
    attend(1, 0)
    attend(1, 1)
    send_needed(3)
    attend(2, 0)
    attend(2, 1)
    for i in range(4):
        to_partner(i).wait_recv()
    attend(3, 0)
    project(0)
    attend(3, 1)
    project(1)
    loads[3].wait()
    loads[4].wait()
    gather_sums(0)
    finish(0)
    gather_sums(1)
    finish(1)

    for c in range(CHUNKS):
        across(c).wait_send()

        @pl.loop(1, PLANE)
        def _(d, c=c):
            first(c, d).wait_send()
            third(c, 0, d).wait_send()
            third(c, 1, d).wait_send()

    for i in range(4):
        to_partner(i).wait_send()
    for s in range(2):
        share(s).wait_send()
        to_near(s).wait_send()
        to_far(s).wait_send()
        to_ahead(s).wait_send()

        @pl.loop(1, 8)
        def _(d, s=s):
            tell(s, d).wait_send()


def local(
    queries, suffix_kv, prefix_kv, out_weight, residual, norm_gain, suffix_len, member, owner, assign
):
    query = jnp.transpose(queries, (0, 2, 1, 3)).reshape(2, 512, 256)
    suffix = suffix_kv.reshape(2, 256, 512)
    prefix = prefix_kv.reshape(PLANE, CHUNKS, ROWS, 512)
    stream = jnp.transpose(residual, (0, 2, 1))
    gain = jnp.broadcast_to(norm_gain[:, None], (COLS, 256))
    smem = pl.BlockSpec(memory_space=pltpu.SMEM)
    anywhere = pl.BlockSpec(memory_space=pl.ANY)
    V = pltpu.VMEM
    DMA = pltpu.SemaphoreType.DMA
    piece = V((PLANE, ROWS, 512), BF)
    pair = [[piece, piece] for _ in range(CHUNKS)]
    out = pl.pallas_call(
        kernel,
        name="prefill",
        out_shape=jax.ShapeDtypeStruct((2, COLS, 256), BF),
        in_specs=[smem] * 4 + [anywhere] * 6,
        out_specs=pl.BlockSpec(memory_space=pltpu.VMEM),
        scratch_shapes=[
            [piece] * CHUNKS, [piece] * CHUNKS, pair, pair,
            V((2, 512, 256), BF), V((2, 256, 512), BF), V((512, D), BF), V((D, 512), BF),
            V((D // 2, 512), BF), V((2, COLS, 256), BF), V((COLS, 256), F32),
            V((2, 512, 256), F32), V((2, 512, 128), F32), V((2, 256, 512), BF), V((2, 256, 512), BF),
            V((2, 3, COLS, 256), BF), V((2, COLS, 256), F32), V((2, COLS, 256), F32),
            V((2, 4, COLS, 256), BF), V((2, 8, 256), F32), V((2, 8, 8, 256), F32),
            pltpu.SMEM((2 * PLANE,), jnp.int32),
            DMA((5,)), DMA((CHUNKS,)), DMA((CHUNKS, PLANE)), DMA((CHUNKS, PLANE)),
            DMA((CHUNKS,)), DMA((CHUNKS,)), DMA((CHUNKS, 2, PLANE)), DMA((CHUNKS, 2, PLANE)),
            DMA((4,)), DMA((4,)), DMA((2,)), DMA((2,)), DMA((2, 3)), DMA((2, 4)),
            DMA((2, 8)), DMA((2, 8)),
        ],
        compiler_params=pltpu.CompilerParams(
            collective_id=0, has_side_effects=True, vmem_limit_bytes=56 * 2**20
        ),
    )(suffix_len, member, owner, assign, query, suffix, prefix, out_weight, stream, gain)
    return jnp.transpose(out, (0, 2, 1))


def solution(mesh):
    in_specs = (
        P("req", None, "tp", None),
        P("req", None, "tp", None),
        P("req", None, "tp", None),
        P("tp", None),
        P("req", None, "tp"),
        P("tp"),
        P(),
        P(),
        P(),
        P(),
    )
    out_specs = P("req", None, "tp")
    return jax.shard_map(local, mesh=mesh, in_specs=in_specs, out_specs=out_specs, check_vma=False)
```

time: 541 us -> 104 us (0.19)
  waiting for transfers between devices: 485 us -> 0 us
  Pallas kernels: 0 us -> 98.2 us
  blocking collectives: 16 us -> 0 us
  between operations: 13.3 us -> 0.01 us
  other arithmetic: 10.5 us -> 0 us
  matrix products: 9.64 us -> 0 us
    reduce_scatter x2 -> x0, waiting for transfers between devices: 307 us -> none  [the longest x1 261 us: total_of(): lax.psum_scatter(padded_to(lines, lax.axis_size(axis)), axis, scatter_dim...]
    all_gather x1 -> x0, waiting for transfers between devices: 178 us -> none  [total_of(): whole = lax.all_gather(own, axis).reshape(-1, *lines.shape[1:])]
    pallas_call x0 -> x1, Pallas kernels: none -> 98.2 us  [local(): pl.pallas_call(kernel, name='prefill', out_shape=jax.ShapeDtypeStruct((2,...]
    psum x1 -> x0, blocking collectives: 16 us -> none  [local(): squares = lax.psum(jnp.sum(mine * mine, -1, keepdims=True), 'tp')]
    dot_general x5 -> x0, matrix products: 9.64 us -> none  [the longest x1 5.95 us: local(): jnp.dot(attended, out_weight, preferred_element_type=jnp.float32)]
    convert_element_type x2 -> x0, other arithmetic: 7.2 us -> none  [the longest x1 6.01 us: local(): placed.astype(jnp.bfloat16)]
  transfers between devices with their start and end apart: 3 -> 0, of which waited for: 3 -> 0; matrix products, arithmetic and copies ran while one was open for 0% -> 0% of each run, Pallas kernels for 0% -> 0%
where the time goes in v1:
time: 104 us; the launch traced here: 103 us
  Pallas kernels  98.2 us (94%)
  local copies, waits for them, and re-layouts  5.29 us (5%)
    pallas_call x1, Pallas kernels, local(): pl.pallas_call(kernel, name='prefill', out_shape=jax.ShapeDtypeStruct((2,...  98.2 us

profile of v1, /device:TPU:1, one launch (start us, length us, event | category | flops | bytes accessed | tf_op | source)
XLA Modules:
  0.0 103.5 jit_solution(9360949590856930931)
XLA Ops:
  0.0 1.6 %broadcast_in_dim.2.gain_hbm = f32[448,256]{1,0:T(8,128)} broadcast(f32[448]{0:T(512)} %param.15), dimensions={0} | broadcast | bytes 460544 | tf_op jit(solution)/shard_map/broadcast_in_dim | solution.py:347
  1.6 1.9 %copy.11 = bf16[2,2,256,256]{3,2,1,0:T(8,128)(2,1)} copy(bf16[2,2,256,256]{3,1,2,0:T(2,128)(2,1)} %bitcast.9) | data formatting | bytes 1048576 | tf_op jit(solution)/shard_map/transpose | solution.py:343
  3.5 98.2 %prefill.1 = bf16[2,448,256]{2,1,0:T(8,128)(2,1)} custom-call(s32[64]{0:T(128)} %suffix_len.1, s32[64]{0:T(128)} %member.1, s32[8]{0:T(128)} %owner.1, s32[64]{0:T(128)} %assign.1, bf16[2,512,256]{2,1,0:T(8,128)(2,1)} %bitcast.6, bf16[2,256,512]{2,1,0:T(8,128)(2,1)} %bitcast.10, bf16[16,4,16,512]{3,2,1,0:T(8,128)(2,1)} %bitcast.8, bf16[512,3584]{1,0:T(8,128)(2,1)} %w_hbm.1, ...), custom_call_target="tpu_custom_call" | custom-call | tf_op jit(solution)/shard_map/prefill/pallas_call | solution.py:354
  101.7 1.8 %copy.13 = bf16[2,256,448]{1,2,0:T(8,128)(2,1)} copy(bf16[2,256,448]{1,2,0:T(8,128)(2,1)} %bitcast.7) | data formatting | bytes 917504

commit v2 on v1

--- a/solution.py
+++ b/solution.py
@@ -7,9 +7,13 @@
 
 D = 3584
 MESH = pl.DeviceIdType.MESH
-CHUNKS = 4
 PLANE = 16
-ROWS = 1024 // PLANE // CHUNKS
+STEPS = [
+    (0, 0), (2, 2), (2, 1), (1, 2), (2, 3), (3, 2), (1, 1), (3, 3),
+    (1, 3), (3, 1), (2, 0), (0, 2), (1, 0), (0, 1), (3, 0), (0, 3),
+]
+CHUNKS = [(0, 16), (16, 16), (32, 16), (48, 16)]
+LAST = len(CHUNKS) - 1
 BF = jnp.bfloat16
 F32 = jnp.float32
 NT = (((1,), (1,)), ((), ()))
@@ -21,7 +25,7 @@
     q_hbm, suf_hbm, pre_hbm, w_hbm, res_hbm, gain_hbm,
     out,
     got, both, out_kv, kv,
-    q, suf, w, wt, wtr, res, gain, acc, tot, att, attr,
+    raw, q, suf, w, wt, wtr, res, gain_row, gain, acc, tot, att, attr,
     part, mid, own, landed, sq, sqr, table,
     local_sem, own_sem, p1s, p1r, zs, zr, p2s, p2r, ws, wr, ats, atr, rs, rr, ss, sr,
 ):
@@ -35,57 +39,52 @@
     partner = tp + 1 - 2 * core
     base = half * PLANE
 
-    def away(d):
-        return (my + d // 4) % 4 * 4 + (mx + d % 4) % 4
+    peers = [(my + dy) % 4 * 4 + (mx + dx) % 4 for dx, dy in STEPS]
 
     def local(i, src, dst):
         return pltpu.make_async_copy(src, dst, local_sem.at[i])
 
     loads = [
-        local(0, q_hbm, q), local(1, suf_hbm, suf), local(2, w_hbm, w),
-        local(3, res_hbm, res), local(4, gain_hbm, gain),
+        local(0, q_hbm, raw), local(1, suf_hbm, suf), local(2, w_hbm, w),
+        local(3, res_hbm, res), local(4, gain_hbm, gain_row),
     ]
 
     barrier = pltpu.get_barrier_semaphore()
-
-    @pl.loop(1, PLANE)
-    def _(d):
-        pl.semaphore_signal(barrier, inc=1, device_id=(base + away(d), tp), device_id_type=MESH)
-
-    @pl.loop(1, 8)
-    def _(d):
-        pl.semaphore_signal(barrier, inc=1, device_id=(req, (tp + d) % 8), device_id_type=MESH)
 
     pl.semaphore_signal(
         barrier, inc=1, device_id=(other_half * PLANE + me, tp), device_id_type=MESH
     )
+    for d in range(1, PLANE):
+        pl.semaphore_signal(barrier, inc=1, device_id=(base + peers[d], tp), device_id_type=MESH)
+    for d in range(1, 8):
+        pl.semaphore_signal(barrier, inc=1, device_id=(req, (tp + d) % 8), device_id_type=MESH)
     for load in loads:
         load.start()
+    def span(c):
+        return pl.ds(*CHUNKS[c])
+
     mine = [
-        pltpu.make_async_copy(pre_hbm.at[me, c], got[c].at[me], own_sem.at[c])
-        for c in range(CHUNKS)
+        pltpu.make_async_copy(pre_hbm.at[me, span(k)], got[k].at[me], own_sem.at[k])
+        for k in range(len(CHUNKS))
     ]
     for copy in mine:
         copy.start()
     pl.semaphore_wait(barrier, 23)
 
-    def first(c, d):
-        to = away(d)
-        return pltpu.make_async_remote_copy(
-            src_ref=pre_hbm.at[to, c], dst_ref=got[c].at[me],
-            send_sem=p1s.at[c, d], recv_sem=p1r.at[c, d],
-            device_id=(base + to, tp), device_id_type=MESH,
-        )
-
-    for c in range(CHUNKS):
-        @pl.loop(1, PLANE)
-        def _(d, c=c):
-            first(c, d).start()
-
-    @pl.loop(0, PLANE)
-    def _(d):
+    def first(k, d):
+        return pltpu.make_async_remote_copy(
+            src_ref=pre_hbm.at[peers[d], span(k)], dst_ref=got[k].at[me],
+            send_sem=p1s.at[k, d], recv_sem=p1r.at[k, d],
+            device_id=(base + peers[d], tp), device_id_type=MESH,
+        )
+
+    for k in range(len(CHUNKS)):
+        for d in range(1, PLANE):
+            first(k, d).start()
+
+    for d in range(PLANE):
         for s in range(2):
-            group = member[assign[(base + away(d)) * 2 + s]] // 8
+            group = member[assign[(base + peers[d]) * 2 + s]] // 8
             apart = owner[group] // PLANE - half
             table[2 * d + s] = group + 8 * apart * apart
 
@@ -98,11 +97,8 @@
 
     def send_across(c):
         mine[c].wait()
-
-        @pl.loop(1, PLANE)
-        def _(d):
+        for d in range(1, PLANE):
             first(c, d).wait_recv()
-
         for g in range(8):
             both[c][g] = got[c][owner[g] % PLANE]
         across(c).start()
@@ -111,21 +107,22 @@
         return pltpu.make_async_remote_copy(
             src_ref=out_kv[c][s].at[d], dst_ref=kv[c][s].at[me],
             send_sem=p2s.at[c, s, d], recv_sem=p2r.at[c, s, d],
-            device_id=(base + away(d), tp), device_id_type=MESH,
-        )
+            device_id=(base + peers[d], tp), device_id_type=MESH,
+        )
+
+    def place(c, s):
+        return (s, 0) if c == LAST else (0, s * CHUNKS[c][1])
 
     def send_needed(c):
         across(c).wait_recv()
         for s in range(2):
-            kv[c][s][me] = both[c][table[s]]
-
-            @pl.loop(1, PLANE)
-            def _(d, s=s):
-                out_kv[c][s][d] = both[c][table[2 * d + s]]
-
-            @pl.loop(1, PLANE)
-            def _(d, s=s):
-                third(c, s, d).start()
+            i, row = place(c, s)
+            kv[c][i][me, row : row + CHUNKS[c][1]] = both[c][table[s]]
+            for d in range(1, PLANE):
+                out_kv[c][i][d, row : row + CHUNKS[c][1]] = both[c][table[2 * d + s]]
+            if s == 1 or i == s and c == LAST:
+                for d in range(1, PLANE):
+                    third(c, i, d).start()
 
     def weigh(s, keys):
         scores = lax.dot_general(q[s], keys, NT, preferred_element_type=F32)
@@ -147,11 +144,12 @@
         tot[s] = lanes(weights)
 
     def attend(c, s):
-        @pl.loop(1, PLANE)
-        def _(d):
-            third(c, s, d).wait_recv()
-
-        both_parts = kv[c][s][...].reshape(PLANE * ROWS, 512)
+        i, row = place(c, s)
+        if i == s:
+            for d in range(1, PLANE):
+                third(c, i, d).wait_recv()
+
+        both_parts = kv[c][i][:, row : row + CHUNKS[c][1]].reshape(-1, 512)
         weights = weigh(s, both_parts[:, :256])
         acc[s] += jnp.dot(weights.astype(BF), both_parts[:, 256:], preferred_element_type=F32)
         tot[s] += lanes(weights)
@@ -164,12 +162,11 @@
             device_id=(req, partner), device_id_type=MESH,
         )
 
-    def turn_weights():
-        loads[2].wait()
-        for i in range(4):
-            wt[896 * i : 896 * (i + 1), :] = w[:, 896 * i : 896 * (i + 1)].T
-        for i in range(4):
-            to_partner(i).start()
+    def turn_weights(i):
+        if i == 0:
+            loads[2].wait()
+        wt[896 * i : 896 * (i + 1), :] = w[:, 896 * i : 896 * (i + 1)].T
+        to_partner(i).start()
 
     def share(s):
         return pltpu.make_async_remote_copy(
@@ -266,7 +263,7 @@
         to_far(s).wait_recv()
         value = own[s] + landed[s, 1].astype(F32) + landed[s, 2].astype(F32)
         own[s] = value
-        sq[s] = jnp.broadcast_to(jnp.sum(value * value, axis=0, keepdims=True), (8, 256))
+        sq[s] = jnp.sum(value * value, axis=0, keepdims=True)
 
         @pl.loop(1, 8)
         def _(d):
@@ -280,49 +277,47 @@
         squares = sq[s]
         for d in range(1, 8):
             squares = squares + sqr[s, d]
-        scale = lax.rsqrt(squares[:1] / D + 1e-06)
+        scale = lax.rsqrt(squares / D + 1e-06)
         out[s] = (res[s].astype(F32) + own[s] * scale * gain[...]).astype(BF)
 
     loads[0].wait()
+    for s in range(2):
+        for h in range(2):
+            q[s, 256 * h : 256 * (h + 1)] = raw[s, :, h, :]
+    loads[4].wait()
+    gain[...] = jnp.broadcast_to(gain_row[...][None, :], (256, COLS)).T
     loads[1].wait()
     attend_suffix(0)
-    send_across(0)
     attend_suffix(1)
-    send_across(1)
-    turn_weights()
-    send_across(2)
-    send_needed(0)
-    send_across(3)
-    send_needed(1)
-    attend(0, 0)
-    attend(0, 1)
-    send_needed(2)
-    attend(1, 0)
-    attend(1, 1)
-    send_needed(3)
-    attend(2, 0)
-    attend(2, 1)
+    for c in range(LAST + 1):
+        send_across(c)
+        for i in range(4):
+            if min(i, LAST) == c:
+                turn_weights(i)
+    for c in range(LAST + 1):
+        send_needed(c)
+        if c >= 1:
+            attend(c - 1, 0)
+            attend(c - 1, 1)
     for i in range(4):
         to_partner(i).wait_recv()
-    attend(3, 0)
+    attend(LAST, 0)
     project(0)
-    attend(3, 1)
+    attend(LAST, 1)
     project(1)
+    for c in range(len(CHUNKS)):
+        across(c).wait_send()
+        for i in range(2 if c == LAST else 1):
+            for d in range(1, PLANE):
+                third(c, i, d).wait_send()
+    for k in range(len(CHUNKS)):
+        for d in range(1, PLANE):
+            first(k, d).wait_send()
     loads[3].wait()
-    loads[4].wait()
     gather_sums(0)
     finish(0)
     gather_sums(1)
     finish(1)
-
-    for c in range(CHUNKS):
-        across(c).wait_send()
-
-        @pl.loop(1, PLANE)
-        def _(d, c=c):
-            first(c, d).wait_send()
-            third(c, 0, d).wait_send()
-            third(c, 1, d).wait_send()
 
     for i in range(4):
         to_partner(i).wait_send()
@@ -340,17 +335,19 @@
 def local(
     queries, suffix_kv, prefix_kv, out_weight, residual, norm_gain, suffix_len, member, owner, assign
 ):
-    query = jnp.transpose(queries, (0, 2, 1, 3)).reshape(2, 512, 256)
     suffix = suffix_kv.reshape(2, 256, 512)
-    prefix = prefix_kv.reshape(PLANE, CHUNKS, ROWS, 512)
+    prefix = prefix_kv.reshape(PLANE, -1, 512)
     stream = jnp.transpose(residual, (0, 2, 1))
-    gain = jnp.broadcast_to(norm_gain[:, None], (COLS, 256))
     smem = pl.BlockSpec(memory_space=pltpu.SMEM)
     anywhere = pl.BlockSpec(memory_space=pl.ANY)
     V = pltpu.VMEM
     DMA = pltpu.SemaphoreType.DMA
-    piece = V((PLANE, ROWS, 512), BF)
-    pair = [[piece, piece] for _ in range(CHUNKS)]
+
+    def piece(rows):
+        return V((PLANE, rows, 512), BF)
+
+    pieces = [piece(rows) for _, rows in CHUNKS]
+    pair = [[piece(2 * rows)] for _, rows in CHUNKS[:-1]] + [[pieces[-1]] * 2]
     out = pl.pallas_call(
         kernel,
         name="prefill",
@@ -358,22 +355,22 @@
         in_specs=[smem] * 4 + [anywhere] * 6,
         out_specs=pl.BlockSpec(memory_space=pltpu.VMEM),
         scratch_shapes=[
-            [piece] * CHUNKS, [piece] * CHUNKS, pair, pair,
-            V((2, 512, 256), BF), V((2, 256, 512), BF), V((512, D), BF), V((D, 512), BF),
-            V((D // 2, 512), BF), V((2, COLS, 256), BF), V((COLS, 256), F32),
+            pieces, pieces, pair, pair,
+            V((2, 256, 2, 256), BF), V((2, 512, 256), BF), V((2, 256, 512), BF), V((512, D), BF), V((D, 512), BF),
+            V((D // 2, 512), BF), V((2, COLS, 256), BF), V((COLS,), F32), V((COLS, 256), F32),
             V((2, 512, 256), F32), V((2, 512, 128), F32), V((2, 256, 512), BF), V((2, 256, 512), BF),
             V((2, 3, COLS, 256), BF), V((2, COLS, 256), F32), V((2, COLS, 256), F32),
-            V((2, 4, COLS, 256), BF), V((2, 8, 256), F32), V((2, 8, 8, 256), F32),
+            V((2, 4, COLS, 256), BF), V((2, 1, 256), F32), V((2, 8, 1, 256), F32),
             pltpu.SMEM((2 * PLANE,), jnp.int32),
-            DMA((5,)), DMA((CHUNKS,)), DMA((CHUNKS, PLANE)), DMA((CHUNKS, PLANE)),
-            DMA((CHUNKS,)), DMA((CHUNKS,)), DMA((CHUNKS, 2, PLANE)), DMA((CHUNKS, 2, PLANE)),
+            DMA((5,)), DMA((LAST + 1,)), DMA((LAST + 1, PLANE)), DMA((LAST + 1, PLANE)),
+            DMA((LAST + 1,)), DMA((LAST + 1,)), DMA((LAST + 1, 2, PLANE)), DMA((LAST + 1, 2, PLANE)),
             DMA((4,)), DMA((4,)), DMA((2,)), DMA((2,)), DMA((2, 3)), DMA((2, 4)),
             DMA((2, 8)), DMA((2, 8)),
         ],
         compiler_params=pltpu.CompilerParams(
             collective_id=0, has_side_effects=True, vmem_limit_bytes=56 * 2**20
         ),
-    )(suffix_len, member, owner, assign, query, suffix, prefix, out_weight, stream, gain)
+    )(suffix_len, member, owner, assign, queries, suffix, prefix, out_weight, stream, norm_gain)
     return jnp.transpose(out, (0, 2, 1))
 
 

time: 104 us -> 96.3 us (0.926)
  Pallas kernels: 98.2 us -> 94.4 us
  local copies, waits for them, and re-layouts: 5.29 us -> 1.82 us
    pallas_call x1, Pallas kernels: 98.2 us -> 94.4 us  [local(): pl.pallas_call(kernel, name='prefill', out_shape=jax.ShapeDtypeStruct((2,...]
    transpose x1 -> x0, local copies, waits for them, and re-layouts: 1.9 us -> none  [local(): query = jnp.transpose(queries, (0, 2, 1, 3)).reshape(2, 512, 256)]
    broadcast_in_dim x1 -> x0, local copies, waits for them, and re-layouts: 1.57 us -> none  [local(): gain = jnp.broadcast_to(norm_gain[:, None], (COLS, 256))]
where the time goes in v2:
time: 96.3 us; the launch traced here: 96.2 us
  Pallas kernels  94.4 us (98%)
  local copies, waits for them, and re-layouts  1.82 us (2%)
    pallas_call x1, Pallas kernels, local(): pl.pallas_call(kernel, name='prefill', out_shape=jax.ShapeDtypeStruct((2,...  94.4 us

profile of v2, /device:TPU:1, one launch (start us, length us, event | category | flops | bytes accessed | tf_op | source)
XLA Modules:
  0.0 96.2 jit_solution(15209041959987461305)
XLA Ops:
  0.0 94.4 %prefill.1 = bf16[2,448,256]{2,1,0:T(8,128)(2,1)} custom-call(s32[64]{0:T(128)} %suffix_len.1, s32[64]{0:T(128)} %member.1, s32[8]{0:T(128)} %owner.1, s32[64]{0:T(128)} %assign.1, bf16[2,256,2,256]{3,2,1,0:T(2,128)(2,1)} %q_hbm.1, bf16[2,256,512]{2,1,0:T(8,128)(2,1)} %bitcast.6, bf16[16,64,512]{2,1,0:T(8,128)(2,1)} %bitcast.5, bf16[512,3584]{1,0:T(8,128)(2,1)} %w_hbm.1, ...), custom_call_target="tpu_custom_call" | custom-call | tf_op jit(solution)/shard_map/prefill/pallas_call | solution.py:351
  94.4 1.8 %copy.12 = bf16[2,256,448]{1,2,0:T(8,128)(2,1)} copy(bf16[2,256,448]{1,2,0:T(8,128)(2,1)} %bitcast.4) | data formatting | bytes 917504

commit v3 on v2

--- a/solution.py
+++ b/solution.py
@@ -14,6 +14,7 @@
 ]
 CHUNKS = [(0, 16), (16, 16), (32, 16), (48, 16)]
 LAST = len(CHUNKS) - 1
+UNITS = [[(0, 0), (0, 1)], [(1, 0), (1, 1)], [(2, 0)], [(3, 0)], [(2, 1), (3, 1)]]
 BF = jnp.bfloat16
 F32 = jnp.float32
 NT = (((1,), (1,)), ((), ()))
@@ -21,11 +22,11 @@
 
 
 def kernel(
-    suffix_len, member, owner, assign,
+    lens_hbm, member_hbm, owner_hbm, assign_hbm,
     q_hbm, suf_hbm, pre_hbm, w_hbm, res_hbm, gain_hbm,
-    out,
+    out_hbm,
     got, both, out_kv, kv,
-    raw, q, suf, w, wt, wtr, res, gain_row, gain, acc, tot, att, attr,
+    suffix_len, member, owner, assign, out, raw, q, suf, w, wt, wtr, res, gain_row, gain, acc, tot, att, attr,
     part, mid, own, landed, sq, sqr, table,
     local_sem, own_sem, p1s, p1r, zs, zr, p2s, p2r, ws, wr, ats, atr, rs, rr, ss, sr,
 ):
@@ -47,6 +48,8 @@
     loads = [
         local(0, q_hbm, raw), local(1, suf_hbm, suf), local(2, w_hbm, w),
         local(3, res_hbm, res), local(4, gain_hbm, gain_row),
+        local(5, lens_hbm, suffix_len), local(6, member_hbm, member), local(7, owner_hbm, owner),
+        local(8, assign_hbm, assign),
     ]
 
     barrier = pltpu.get_barrier_semaphore()
@@ -82,6 +85,9 @@
         for d in range(1, PLANE):
             first(k, d).start()
 
+    for load in loads[5:]:
+        load.wait()
+
     for d in range(PLANE):
         for s in range(2):
             group = member[assign[(base + peers[d]) * 2 + s]] // 8
@@ -103,26 +109,29 @@
             both[c][g] = got[c][owner[g] % PLANE]
         across(c).start()
 
-    def third(c, s, d):
-        return pltpu.make_async_remote_copy(
-            src_ref=out_kv[c][s].at[d], dst_ref=kv[c][s].at[me],
-            send_sem=p2s.at[c, s, d], recv_sem=p2r.at[c, s, d],
+    def third(u, d):
+        return pltpu.make_async_remote_copy(
+            src_ref=out_kv[u].at[d], dst_ref=kv[u].at[me],
+            send_sem=p2s.at[u, d], recv_sem=p2r.at[u, d],
             device_id=(base + peers[d], tp), device_id_type=MESH,
         )
 
     def place(c, s):
-        return (s, 0) if c == LAST else (0, s * CHUNKS[c][1])
+        for u, parts in enumerate(UNITS):
+            if (c, s) in parts:
+                row = sum(CHUNKS[k][1] for k, _ in parts[: parts.index((c, s))])
+                return u, slice(row, row + CHUNKS[c][1])
 
     def send_needed(c):
         across(c).wait_recv()
         for s in range(2):
-            i, row = place(c, s)
-            kv[c][i][me, row : row + CHUNKS[c][1]] = both[c][table[s]]
+            u, rows = place(c, s)
+            kv[u][me, rows] = both[c][table[s]]
             for d in range(1, PLANE):
-                out_kv[c][i][d, row : row + CHUNKS[c][1]] = both[c][table[2 * d + s]]
-            if s == 1 or i == s and c == LAST:
+                out_kv[u][d, rows] = both[c][table[2 * d + s]]
+            if UNITS[u][-1] == (c, s):
                 for d in range(1, PLANE):
-                    third(c, i, d).start()
+                    third(u, d).start()
 
     def weigh(s, keys):
         scores = lax.dot_general(q[s], keys, NT, preferred_element_type=F32)
@@ -144,12 +153,12 @@
         tot[s] = lanes(weights)
 
     def attend(c, s):
-        i, row = place(c, s)
-        if i == s:
+        u, rows = place(c, s)
+        if UNITS[u][0] == (c, s):
             for d in range(1, PLANE):
-                third(c, i, d).wait_recv()
-
-        both_parts = kv[c][i][:, row : row + CHUNKS[c][1]].reshape(-1, 512)
+                third(u, d).wait_recv()
+
+        both_parts = kv[u][:, rows].reshape(-1, 512)
         weights = weigh(s, both_parts[:, :256])
         acc[s] += jnp.dot(weights.astype(BF), both_parts[:, 256:], preferred_element_type=F32)
         tot[s] += lanes(weights)
@@ -279,40 +288,52 @@
             squares = squares + sqr[s, d]
         scale = lax.rsqrt(squares / D + 1e-06)
         out[s] = (res[s].astype(F32) + own[s] * scale * gain[...]).astype(BF)
-
-    loads[0].wait()
-    for s in range(2):
-        for h in range(2):
-            q[s, 256 * h : 256 * (h + 1)] = raw[s, :, h, :]
-    loads[4].wait()
-    gain[...] = jnp.broadcast_to(gain_row[...][None, :], (256, COLS)).T
-    loads[1].wait()
+        local(9 + s, out.at[s], out_hbm.at[s]).start()
+
+    def prepare():
+        loads[0].wait()
+        for s in range(2):
+            for h in range(2):
+                q[s, 256 * h : 256 * (h + 1)] = raw[s, :, h, :]
+        loads[4].wait()
+        gain[...] = jnp.broadcast_to(gain_row[...][None, :], (256, COLS)).T
+        loads[1].wait()
+
+    prepare()
     attend_suffix(0)
+    send_across(0)
     attend_suffix(1)
-    for c in range(LAST + 1):
-        send_across(c)
-        for i in range(4):
-            if min(i, LAST) == c:
-                turn_weights(i)
-    for c in range(LAST + 1):
-        send_needed(c)
-        if c >= 1:
-            attend(c - 1, 0)
-            attend(c - 1, 1)
+    send_across(1)
+    turn_weights(0)
+    send_across(2)
+    turn_weights(1)
+    send_across(3)
+    send_needed(0)
+    turn_weights(2)
+    turn_weights(3)
+    send_needed(1)
+    attend(0, 0)
+    attend(0, 1)
+    send_needed(2)
+    attend(1, 0)
+    attend(1, 1)
+    send_needed(3)
+    attend(2, 0)
     for i in range(4):
         to_partner(i).wait_recv()
-    attend(LAST, 0)
+    attend(3, 0)
     project(0)
-    attend(LAST, 1)
+    attend(2, 1)
+    attend(3, 1)
     project(1)
     for c in range(len(CHUNKS)):
         across(c).wait_send()
-        for i in range(2 if c == LAST else 1):
-            for d in range(1, PLANE):
-                third(c, i, d).wait_send()
     for k in range(len(CHUNKS)):
         for d in range(1, PLANE):
             first(k, d).wait_send()
+    for u in range(len(UNITS)):
+        for d in range(1, PLANE):
+            third(u, d).wait_send()
     loads[3].wait()
     gather_sums(0)
     finish(0)
@@ -331,6 +352,8 @@
         def _(d, s=s):
             tell(s, d).wait_send()
 
+        local(9 + s, out.at[s], out_hbm.at[s]).wait()
+
 
 def local(
     queries, suffix_kv, prefix_kv, out_weight, residual, norm_gain, suffix_len, member, owner, assign
@@ -338,7 +361,6 @@
     suffix = suffix_kv.reshape(2, 256, 512)
     prefix = prefix_kv.reshape(PLANE, -1, 512)
     stream = jnp.transpose(residual, (0, 2, 1))
-    smem = pl.BlockSpec(memory_space=pltpu.SMEM)
     anywhere = pl.BlockSpec(memory_space=pl.ANY)
     V = pltpu.VMEM
     DMA = pltpu.SemaphoreType.DMA
@@ -347,23 +369,24 @@
         return V((PLANE, rows, 512), BF)
 
     pieces = [piece(rows) for _, rows in CHUNKS]
-    pair = [[piece(2 * rows)] for _, rows in CHUNKS[:-1]] + [[pieces[-1]] * 2]
+    units = [piece(sum(CHUNKS[c][1] for c, _ in parts)) for parts in UNITS]
     out = pl.pallas_call(
         kernel,
         name="prefill",
         out_shape=jax.ShapeDtypeStruct((2, COLS, 256), BF),
-        in_specs=[smem] * 4 + [anywhere] * 6,
-        out_specs=pl.BlockSpec(memory_space=pltpu.VMEM),
+        in_specs=[anywhere] * 10,
+        out_specs=anywhere,
         scratch_shapes=[
-            pieces, pieces, pair, pair,
-            V((2, 256, 2, 256), BF), V((2, 512, 256), BF), V((2, 256, 512), BF), V((512, D), BF), V((D, 512), BF),
+            pieces, pieces, units, units,
+            pltpu.SMEM((64,), jnp.int32), pltpu.SMEM((64,), jnp.int32), pltpu.SMEM((8,), jnp.int32),
+            pltpu.SMEM((64,), jnp.int32), V((2, COLS, 256), BF), V((2, 256, 2, 256), BF), V((2, 512, 256), BF), V((2, 256, 512), BF), V((512, D), BF), V((D, 512), BF),
             V((D // 2, 512), BF), V((2, COLS, 256), BF), V((COLS,), F32), V((COLS, 256), F32),
             V((2, 512, 256), F32), V((2, 512, 128), F32), V((2, 256, 512), BF), V((2, 256, 512), BF),
             V((2, 3, COLS, 256), BF), V((2, COLS, 256), F32), V((2, COLS, 256), F32),
             V((2, 4, COLS, 256), BF), V((2, 1, 256), F32), V((2, 8, 1, 256), F32),
             pltpu.SMEM((2 * PLANE,), jnp.int32),
-            DMA((5,)), DMA((LAST + 1,)), DMA((LAST + 1, PLANE)), DMA((LAST + 1, PLANE)),
-            DMA((LAST + 1,)), DMA((LAST + 1,)), DMA((LAST + 1, 2, PLANE)), DMA((LAST + 1, 2, PLANE)),
+            DMA((11,)), DMA((LAST + 1,)), DMA((LAST + 1, PLANE)), DMA((LAST + 1, PLANE)),
+            DMA((LAST + 1,)), DMA((LAST + 1,)), DMA((len(UNITS), PLANE)), DMA((len(UNITS), PLANE)),
             DMA((4,)), DMA((4,)), DMA((2,)), DMA((2,)), DMA((2, 3)), DMA((2, 4)),
             DMA((2, 8)), DMA((2, 8)),
         ],

time: 96.3 us -> 93.6 us (0.972)
  Pallas kernels: 94.4 us -> 91.7 us
    pallas_call x1, Pallas kernels: 94.4 us -> 91.7 us  [local(): pl.pallas_call(kernel, name='prefill', out_shape=jax.ShapeDtypeStruct((2,...]
where the time goes in v3:
time: 93.6 us; the launch traced here: 93.5 us
  Pallas kernels  91.7 us (98%)
  local copies, waits for them, and re-layouts  1.82 us (2%)
    pallas_call x1, Pallas kernels, local(): pl.pallas_call(kernel, name='prefill', out_shape=jax.ShapeDtypeStruct((2,...  91.7 us

profile of v3, /device:TPU:1, one launch (start us, length us, event | category | flops | bytes accessed | tf_op | source)
XLA Modules:
  0.0 93.5 jit_solution(6323283143624548400)
XLA Ops:
  0.0 91.7 %prefill.1 = bf16[2,448,256]{2,1,0:T(8,128)(2,1)} custom-call(s32[64]{0:T(128)} %lens_hbm.1, s32[64]{0:T(128)} %member_hbm.1, s32[8]{0:T(128)} %owner_hbm.1, s32[64]{0:T(128)} %assign_hbm.1, bf16[2,256,2,256]{3,2,1,0:T(2,128)(2,1)} %q_hbm.1, bf16[2,256,512]{2,1,0:T(8,128)(2,1)} %bitcast.6, bf16[16,64,512]{2,1,0:T(8,128)(2,1)} %bitcast.5, ...), custom_call_target="tpu_custom_call" | custom-call | tf_op jit(solution)/shard_map/prefill/pallas_call | solution.py:373
  91.7 1.8 %copy.12 = bf16[2,256,448]{1,2,0:T(8,128)(2,1)} copy(bf16[2,256,448]{1,2,0:T(8,128)(2,1)} %bitcast.4) | data formatting | bytes 917504

commit v4 on v3

--- a/solution.py
+++ b/solution.py
@@ -24,9 +24,9 @@
 def kernel(
     lens_hbm, member_hbm, owner_hbm, assign_hbm,
     q_hbm, suf_hbm, pre_hbm, w_hbm, res_hbm, gain_hbm,
-    out_hbm,
+    out,
     got, both, out_kv, kv,
-    suffix_len, member, owner, assign, out, raw, q, suf, w, wt, wtr, res, gain_row, gain, acc, tot, att, attr,
+    suffix_len, member, owner, assign, raw, q, suf, w, wt, wtr, res, gain_row, gain, acc, tot, att, attr,
     part, mid, own, landed, sq, sqr, table,
     local_sem, own_sem, p1s, p1r, zs, zr, p2s, p2r, ws, wr, ats, atr, rs, rr, ss, sr,
 ):
@@ -288,7 +288,6 @@
             squares = squares + sqr[s, d]
         scale = lax.rsqrt(squares / D + 1e-06)
         out[s] = (res[s].astype(F32) + own[s] * scale * gain[...]).astype(BF)
-        local(9 + s, out.at[s], out_hbm.at[s]).start()
 
     def prepare():
         loads[0].wait()
@@ -352,8 +351,6 @@
         def _(d, s=s):
             tell(s, d).wait_send()
 
-        local(9 + s, out.at[s], out_hbm.at[s]).wait()
-
 
 def local(
     queries, suffix_kv, prefix_kv, out_weight, residual, norm_gain, suffix_len, member, owner, assign
@@ -373,19 +370,19 @@
     out = pl.pallas_call(
         kernel,
         name="prefill",
-        out_shape=jax.ShapeDtypeStruct((2, COLS, 256), BF),
+        out_shape=pltpu.VMEM((2, COLS, 256), BF),
         in_specs=[anywhere] * 10,
-        out_specs=anywhere,
+        out_specs=pl.BlockSpec(memory_space=pltpu.VMEM),
         scratch_shapes=[
             pieces, pieces, units, units,
             pltpu.SMEM((64,), jnp.int32), pltpu.SMEM((64,), jnp.int32), pltpu.SMEM((8,), jnp.int32),
-            pltpu.SMEM((64,), jnp.int32), V((2, COLS, 256), BF), V((2, 256, 2, 256), BF), V((2, 512, 256), BF), V((2, 256, 512), BF), V((512, D), BF), V((D, 512), BF),
+            pltpu.SMEM((64,), jnp.int32), V((2, 256, 2, 256), BF), V((2, 512, 256), BF), V((2, 256, 512), BF), V((512, D), BF), V((D, 512), BF),
             V((D // 2, 512), BF), V((2, COLS, 256), BF), V((COLS,), F32), V((COLS, 256), F32),
             V((2, 512, 256), F32), V((2, 512, 128), F32), V((2, 256, 512), BF), V((2, 256, 512), BF),
             V((2, 3, COLS, 256), BF), V((2, COLS, 256), F32), V((2, COLS, 256), F32),
             V((2, 4, COLS, 256), BF), V((2, 1, 256), F32), V((2, 8, 1, 256), F32),
             pltpu.SMEM((2 * PLANE,), jnp.int32),
-            DMA((11,)), DMA((LAST + 1,)), DMA((LAST + 1, PLANE)), DMA((LAST + 1, PLANE)),
+            DMA((9,)), DMA((LAST + 1,)), DMA((LAST + 1, PLANE)), DMA((LAST + 1, PLANE)),
             DMA((LAST + 1,)), DMA((LAST + 1,)), DMA((len(UNITS), PLANE)), DMA((len(UNITS), PLANE)),
             DMA((4,)), DMA((4,)), DMA((2,)), DMA((2,)), DMA((2, 3)), DMA((2, 4)),
             DMA((2, 8)), DMA((2, 8)),

time: 93.6 us -> 91.9 us (0.982)
  local copies, waits for them, and re-layouts: 1.82 us -> 0.77 us
    unnamed x1, local copies, waits for them, and re-layouts: 1.82 us -> 0.77 us
where the time goes in v4:
time: 91.9 us; the launch traced here: 91.8 us
  Pallas kernels  91 us (99%)
    pallas_call x1, Pallas kernels, local(): pl.pallas_call(kernel, name='prefill', out_shape=pltpu.VMEM((2, COLS, 256...  91 us

profile of v4, /device:TPU:1, one launch (start us, length us, event | category | flops | bytes accessed | tf_op | source)
XLA Modules:
  0.0 91.8 jit_solution(994396873909318886)
XLA Ops:
  0.0 91.0 %prefill.1 = bf16[2,448,256]{2,1,0:T(8,128)(2,1)S(1)} custom-call(s32[64]{0:T(128)} %lens_hbm.1, s32[64]{0:T(128)} %member_hbm.1, s32[8]{0:T(128)} %owner_hbm.1, s32[64]{0:T(128)} %assign_hbm.1, bf16[2,256,2,256]{3,2,1,0:T(2,128)(2,1)} %q_hbm.1, bf16[2,256,512]{2,1,0:T(8,128)(2,1)} %bitcast.6, bf16[16,64,512]{2,1,0:T(8,128)(2,1)} %bitcast.5, ...), custom_call_target="tpu_custom_call" | custom-call | tf_op jit(solution)/shard_map/prefill/pallas_call | solution.py:370
  91.1 0.8 copy.12

commit v5 on v4

--- a/solution.py
+++ b/solution.py
@@ -40,7 +40,10 @@
     partner = tp + 1 - 2 * core
     base = half * PLANE
 
-    peers = [(my + dy) % 4 * 4 + (mx + dx) % 4 for dx, dy in STEPS]
+    peers = [
+        (my + dy + core * (dx - dy) + 4) % 4 * 4 + (mx + dx + core * (dy - dx) + 4) % 4
+        for dx, dy in STEPS
+    ]
 
     def local(i, src, dst):
         return pltpu.make_async_copy(src, dst, local_sem.at[i])

time: 91.9 us -> 91.8 us (level)
  no operation moved by 1% of the time
where the time goes in v5:
time: 91.8 us; the launch traced here: 91.7 us
  Pallas kernels  90.9 us (99%)
    pallas_call x1, Pallas kernels, local(): pl.pallas_call(kernel, name='prefill', out_shape=pltpu.VMEM((2, COLS, 256...  90.9 us

profile of v5, /device:TPU:1, one launch (start us, length us, event | category | flops | bytes accessed | tf_op | source)
XLA Modules:
  0.0 91.7 jit_solution(15977009797119368192)
XLA Ops:
  0.0 90.9 %prefill.1 = bf16[2,448,256]{2,1,0:T(8,128)(2,1)S(1)} custom-call(s32[64]{0:T(128)} %lens_hbm.1, s32[64]{0:T(128)} %member_hbm.1, s32[8]{0:T(128)} %owner_hbm.1, s32[64]{0:T(128)} %assign_hbm.1, bf16[2,256,2,256]{3,2,1,0:T(2,128)(2,1)} %q_hbm.1, bf16[2,256,512]{2,1,0:T(8,128)(2,1)} %bitcast.6, bf16[16,64,512]{2,1,0:T(8,128)(2,1)} %bitcast.5, ...), custom_call_target="tpu_custom_call" | custom-call | tf_op jit(solution)/shard_map/prefill/pallas_call | solution.py:373
  91.0 0.8 copy.12

commit v6 on v5

--- a/solution.py
+++ b/solution.py
@@ -272,8 +272,9 @@
             own[s] += landed[s, 3].astype(F32)
 
         to_near(s).wait_recv()
+        own[s] += landed[s, 1].astype(F32)
         to_far(s).wait_recv()
-        value = own[s] + landed[s, 1].astype(F32) + landed[s, 2].astype(F32)
+        value = own[s] + landed[s, 2].astype(F32)
         own[s] = value
         sq[s] = jnp.sum(value * value, axis=0, keepdims=True)
 

time: 91.8 us -> 91.8 us (level)
  no operation moved by 1% of the time
where the time goes in v6:
time: 91.8 us; the launch traced here: 91.7 us
  Pallas kernels  91 us (99%)
    pallas_call x1, Pallas kernels, local(): pl.pallas_call(kernel, name='prefill', out_shape=pltpu.VMEM((2, COLS, 256...  91 us

profile of v6, /device:TPU:1, one launch (start us, length us, event | category | flops | bytes accessed | tf_op | source)
XLA Modules:
  0.0 91.7 jit_solution(17444417635018255426)
XLA Ops:
  0.0 91.0 %prefill.1 = bf16[2,448,256]{2,1,0:T(8,128)(2,1)S(1)} custom-call(s32[64]{0:T(128)} %lens_hbm.1, s32[64]{0:T(128)} %member_hbm.1, s32[8]{0:T(128)} %owner_hbm.1, s32[64]{0:T(128)} %assign_hbm.1, bf16[2,256,2,256]{3,2,1,0:T(2,128)(2,1)} %q_hbm.1, bf16[2,256,512]{2,1,0:T(8,128)(2,1)} %bitcast.6, bf16[16,64,512]{2,1,0:T(8,128)(2,1)} %bitcast.5, ...), custom_call_target="tpu_custom_call" | custom-call | tf_op jit(solution)/shard_map/prefill/pallas_call | solution.py:374
  91.0 0.8 copy.12
